TPU v7x, 32 devices: a whole 2x2x4 slice. The times are simulated.
32 devices in a mesh: tile: 4 (over z), chan: 4 (over y, x), tm: 2 (over core).
Axes of the slice: x: 2, y: 2, z: 4, core: 2. Of those that a mesh axis runs over, the one named last changes fastest.
Arguments:
- observed_values: bfloat16 [2, 65536, 128], P('tm', ('tile', 'chan')), may hold values from -6 to 6
- observed_tile: int32 [2, 65536, 1], P('tm', ('tile', 'chan')), may hold values from 0 to 3; in each aligned block of 4096 rows (0 to 4095, 4096 to 8191, ..., all dimensions but the last counted through in order) at most 2048 rows name the same one
- observed_cell: int32 [2, 65536], P('tm', ('tile', 'chan')), may hold values from 0 to 2047
- patch_weight: bfloat16 [4, 256, 256], P(None, None, 'chan'), may hold values from -0.1875 to 0.1875
- depth_weight: bfloat16 [9, 256], P(None, 'chan'), may hold values from -2 to 2
- owners: int32 [4, 4], replicated, may hold values from 0 to 3, as said below
Outputs:
- owned: bfloat16 [4, 2, 4, 64, 256], P('tile', 'tm', None, None, 'chan')
Inputs may be any that keep to these rules, and one draw needn't show every extreme that they name: `observed_tile`: in the rows of one device at most 2048 name the same tile. owners[t, j] - t is the same modulo 4 for every t and differs between any two j, so every row and every column of owners is a permutation.
All inputs are finite; a program needn't handle non-finite values.
Results may differ from a plain program's by a relative error of at most 0.014.
Values may be sent and summed in bfloat16 or wider, within the bound.
A program may use at most 64 MiB of HBM per device.

v0:
```python
import jax
import jax.numpy as jnp
from jax import lax
from jax.sharding import PartitionSpec as P

V = 128
HS = 32
WS = 64


def padded(x, sides, width):
    for axis, dim in sides:
        devices, length = (lax.axis_size(axis), x.shape[dim])
        up = [(i, (i + 1) % devices) for i in range(devices - 1)]
        down = [(j, i) for i, j in up]
        last = lax.slice_in_dim(x, length - width, length, axis=dim)
        first = lax.slice_in_dim(x, 0, width, axis=dim)
        before = lax.ppermute(last, axis, up)
        after = lax.ppermute(first, axis, down)
        x = jnp.concatenate([before, x, after], axis=dim)
    return x


def pack_rows(values, destination, placed, tile_count, capacity):
    match = (destination[:, None] == lax.iota(jnp.int32, tile_count)[None, :]).astype(jnp.int32)
    earlier = jnp.cumsum(match, axis=0) - match
    position = jnp.sum(earlier * match, axis=1)
    slot_index = destination * capacity + position
    width = values.shape[1]
    sent_values = jnp.zeros((tile_count * capacity, width), jnp.bfloat16).at[slot_index].set(values)
    sent_cells = jnp.full((tile_count * capacity,), -1, jnp.int32).at[slot_index].set(placed)
    return (
        sent_values.reshape(tile_count, capacity, width),
        sent_cells.reshape(tile_count, capacity),
    )


def grid_block(arrived_values, arrived_cells, first_cell):
    cell_ids = first_cell + lax.iota(jnp.int32, 128)
    matches = cell_ids[:, None] == arrived_cells[None, :]
    totals = jnp.dot(
        matches.astype(jnp.bfloat16), arrived_values, preferred_element_type=jnp.float32
    )
    counts = jnp.sum(matches.astype(jnp.float32), axis=1)
    return (totals, counts)


def patch_rows(field, weight, row_start, row_count):
    slab = lax.dynamic_slice_in_dim(field, 2 * row_start, 2 * row_count, 0)
    depth_in = field.shape[2]
    result = jnp.zeros((row_count * (field.shape[1] // 2), weight.shape[2]), jnp.float32)
    for tap_row in range(2):
        for tap_col in range(2):
            window = slab[tap_row::2, tap_col::2, :].reshape(-1, depth_in)
            result = result + jnp.dot(
                window, weight[tap_row * 2 + tap_col], preferred_element_type=jnp.float32
            )
    return result.reshape(row_count, field.shape[1] // 2, weight.shape[2])


def local(observed_values, observed_tile, observed_cell, patch_weight, depth_weight, owners):
    tile_count = lax.axis_size("tile")
    slot_count = lax.axis_size("tm")
    values = observed_values[0]
    capacity = 2 * values.shape[0] // tile_count
    sent_values, sent_cells = pack_rows(
        values, observed_tile[0, :, 0], observed_cell[0], tile_count, capacity
    )
    arrived = (
        lax.all_to_all(sent_values, "tile", split_axis=0, concat_axis=0, tiled=True),
        lax.all_to_all(sent_cells, "tile", split_axis=0, concat_axis=0, tiled=True),
    )
    arrived_values = arrived[0].reshape(-1, V)
    arrived_cells = arrived[1].reshape(-1)
    cell_count = HS * WS
    firsts = jnp.arange(cell_count // 128, dtype=jnp.int32) * 128
    totals, counts = lax.map(
        lambda first_cell: grid_block(arrived_values, arrived_cells, first_cell), firsts
    )
    totals = totals.reshape(cell_count, V)
    counts = counts.reshape(cell_count)
    totals, counts = (
        lax.psum(totals.astype(jnp.bfloat16), "chan").astype(jnp.float32),
        lax.psum(counts.astype(jnp.bfloat16), "chan").astype(jnp.float32),
    )
    means = (totals / jnp.maximum(counts, 1.0)[:, None]).astype(jnp.bfloat16)
    means = means.reshape(HS, WS, V)
    out_rows = HS // (2 * slot_count)
    half_cols = WS // 2
    stacked = lax.all_gather(means, "tm", axis=2, tiled=True)
    encoded = patch_rows(stacked, patch_weight, lax.axis_index("tm") * out_rows, out_rows)
    hidden = jax.nn.gelu(encoded).astype(jnp.bfloat16)
    rimmed = padded(hidden, ((("tile", "tm"), 0),), 2)
    widened = jnp.pad(rimmed, ((0, 0), (2, 2), (0, 0))).astype(jnp.float32)
    depth = jnp.zeros(hidden.shape, jnp.float32)
    for tap_row in range(3):
        for tap_col in range(3):
            shifted = widened[
                2 * tap_row : 2 * tap_row + out_rows, 2 * tap_col : 2 * tap_col + half_cols, :
            ]
            depth = depth + shifted * depth_weight[tap_row * 3 + tap_col].astype(jnp.float32)
    latent = (hidden.astype(jnp.float32) + depth).astype(jnp.bfloat16)
    channels = latent.shape[2]
    pieces = latent.reshape(tile_count, -1, channels)
    own_row = lax.dynamic_index_in_dim(owners, lax.axis_index("tile"), 0, keepdims=False)
    order = lax.iota(jnp.int32, tile_count)
    chosen = jnp.sum(
        order[None, :] * (own_row[None, :] == order[:, None]).astype(jnp.int32), axis=1
    )
    outgoing = pieces[chosen]
    received = lax.all_to_all(outgoing, "tile", split_axis=0, concat_axis=0, tiled=True)
    return received.reshape(1, 1, tile_count, -1, channels)


def solution(mesh):
    placed = (
        P("tm", ("tile", "chan"), None),
        P("tm", ("tile", "chan"), None),
        P("tm", ("tile", "chan")),
        P(None, None, "chan"),
        P(None, "chan"),
        P(),
    )
    return jax.shard_map(
        local,
        mesh=mesh,
        in_specs=placed,
        out_specs=P("tile", "tm", None, None, "chan"),
        check_vma=False,
    )
```

profile of v0, /device:TPU:0, one launch (start us, length us, event | category | flops | bytes accessed | tf_op | source)
XLA Modules:
  0.0 239.9 jit_solution(12376599636071230112)
XLA Ops:
  10.6 16.3 %scatter_custom_fusion = s32[8192]{0:T(1024)} fusion(s32[4096]{0:T(1024)S(1)} %bitcast.137, s32[4096]{0:T(1024)} %bitcast.141, s32[]{:T(128)} %constant.27.clone.1), kind=kCustom, calls=%fused_computation.77 | custom fusion | bytes 33280 | tf_op jit(solution)/shard_map/scatter | solution.py:31
  26.9 6.3 %all-to-all-start = ((s32[4,1,2048]{2,1,0:T(1,128)}), s32[4,1,2048]{2,1,0:T(1,128)S(1)}, u32[]{:S(2)}, u32[]{:S(2)}) async-start(s32[4,1,2048]{2,1,0:T(1,128)} %bitcast.10), calls=%async_computation | async-start | bytes 65536 | tf_op jit(solution)/shard_map/all_to_all | solution.py:71
  33.2 12.4 %scatter_custom_fusion.1 = bf16[8192,128]{1,0:T(8,128)(2,1)} fusion(s32[4096]{0:T(1024)S(1)} %bitcast.138, bf16[1,4096,128]{2,1,0:T(8,128)(2,1)S(1)} %copy-done, bf16[]{:T(256)} %constant.19.clone.1), kind=kCustom, calls=%fused_computation.15 | custom fusion | bytes 3145730 | tf_op jit(solution)/shard_map/scatter | solution.py:30
  45.6 5.1 %all-to-all-start.1 = ((bf16[4,2048,128]{2,1,0:T(8,128)(2,1)}), bf16[4,2048,128]{2,1,0:T(8,128)(2,1)S(1)}, u32[]{:S(2)}, u32[]{:S(2)}) async-start(bf16[4,2048,128]{2,1,0:T(8,128)(2,1)} %bitcast.12), calls=%async_computation.1 | async-start | bytes 4194304 | tf_op jit(solution)/shard_map/all_to_all | solution.py:70
  50.8 47.6 %all-to-all-done.1 = bf16[4,2048,128]{2,1,0:T(8,128)(2,1)S(1)} async-done(((bf16[4,2048,128]{2,1,0:T(8,128)(2,1)}), bf16[4,2048,128]{2,1,0:T(8,128)(2,1)S(1)}, u32[]{:S(2)}, u32[]{:S(2)}) %all-to-all-start.1) | async-done | bytes 2097184 | tf_op jit(solution)/shard_map/all_to_all | solution.py:70
  98.4 56.3 %while.12 = (s32[]{:T(128)}, bf16[16,128,128]{2,1,0:T(8,128)(2,1)}, bf16[16,128]{1,0:T(8,128)(2,1)S(1)}, s32[16]{0:T(128)S(1)}, s32[4,2048]{1,0:T(4,128)S(1)}, /...) while((s32[]{:T(128)}, bf16[16,128,128]{2,1,0:T(8,128)(2,1)}, bf16[16,128]{1,0:T(8,128)(2,1)S(1)}, ...), condition=%wide.region_7.8_spmd, body=%wide.region_5.7_spmd.sunk | while | flops 272629760 | bytes 2296681 | solution.py:77
  99.7 1.5 fusion.67
  103.3 1.5 fusion.67
  106.8 1.5 fusion.67
  117.3 1.5 fusion.67
  120.9 1.5 fusion.67
  124.4 1.5 fusion.67
  131.4 1.5 fusion.67
  134.9 1.5 fusion.67
  138.5 1.5 fusion.67
  145.5 1.5 fusion.67
  152.5 1.5 fusion.67
  154.8 10.1 %psum.15 = bf16[2048]{0:T(1024)(128)(2,1)S(1)} all-reduce(bf16[2048]{0:T(1024)(128)(2,1)S(1)} %bitcast.140), channel_id=1, replica_groups=mesh['tile'=4,'chan'=4,'tm'=2] {'chan'}, use_global_device_ids=true, to_apply=%region_9.10 | all-reduce | flops 2048 | bytes 8192 | tf_op jit(solution)/shard_map/psum | solution.py:84
  164.9 34.5 %all-reduce.3.cloned.1.call-done = bf16[2048,128]{1,0:T(8,128)(2,1)} async-done(((bf16[2048,128]{1,0:T(8,128)(2,1)}), bf16[2048,128]{1,0:T(8,128)(2,1)}) %all-reduce.3.cloned.1.call-update) | async-done | bytes 524304 | tf_op jit(solution)/shard_map/psum | solution.py:83
  199.4 2.2 divide_convert_fusion
  202.5 8.1 %all-gather.2.cloned.1.call-done = bf16[32,64,256]{2,1,0:T(8,128)(2,1)} async-done(((bf16[32,64,128]{2,1,0:T(8,128)(2,1)}), bf16[32,64,256]{2,1,0:T(8,128)(2,1)}) %all-gather.2.cloned.1.call-update) | async-done | bytes 1048592 | tf_op jit(solution)/shard_map/all_gather | solution.py:90
  214.1 2.2 collective-permute-start
  217.6 2.9 %collective-permute-done.1 = bf16[2,32,64]{2,1,0:T(8,128)(2,1)S(1)} collective-permute-done((bf16[2,32,64]{2,1,0:T(8,128)(2,1)S(1)}, bf16[2,32,64]{2,1,0:T(8,128)(2,1)S(1)}, u32[]{:S(2)}, u32[]{:S(2)}) %collective-permute-start.1) | collective-permute-done | bytes 8224 | tf_op jit(solution)/shard_map/ppermute | solution.py:19
  221.4 11.0 %all_to_all.22 = bf16[4,2,2048]{2,1,0:T(2,128)(2,1)S(1)} all-to-all(bf16[4,2,2048]{2,1,0:T(2,128)(2,1)S(1)} %reshape.214), channel_id=1, replica_groups=mesh['tile'=4,'chan'=4,'tm'=2] {'tile'}, dimensions={0} | all-to-all | bytes 65536 | tf_op jit(solution)/shard_map/all_to_all | solution.py:111
  (132 shorter events, 51.0 us)
Async XLA Ops:
  6.5 26.7 %copy-start = (bf16[1,4096,128]{2,1,0:T(8,128)(2,1)S(1)}, bf16[1,4096,128]{2,1,0:T(8,128)(2,1)}, u32[]{:S(2)}) copy-start(bf16[1,4096,128]{2,1,0:T(8,128)(2,1)} %param.8) | copy-start | bytes 3145732
  26.9 18.8 %all-to-all-start = ((s32[4,1,2048]{2,1,0:T(1,128)}), s32[4,1,2048]{2,1,0:T(1,128)S(1)}, u32[]{:S(2)}, u32[]{:S(2)}) async-start(s32[4,1,2048]{2,1,0:T(1,128)} %bitcast.10), calls=%async_computation | async-start | bytes 65536 | tf_op jit(solution)/shard_map/all_to_all | solution.py:71
  45.6 52.7 %all-to-all-start.1 = ((bf16[4,2048,128]{2,1,0:T(8,128)(2,1)}), bf16[4,2048,128]{2,1,0:T(8,128)(2,1)S(1)}, u32[]{:S(2)}, u32[]{:S(2)}) async-start(bf16[4,2048,128]{2,1,0:T(8,128)(2,1)} %bitcast.12), calls=%async_computation.1 | async-start | bytes 4194304 | tf_op jit(solution)/shard_map/all_to_all | solution.py:70
  50.7 148.7 %all-reduce.3.cloned.1.call-start = ((), (), s32[]{:S(2)}) async-start(), calls=%async_computation.3 | async-start | bytes 1048576 | tf_op jit(solution)/shard_map/psum | solution.py:83
  154.7 47.8 %copy-start.2 = (bf16[9,64]{1,0:T(8,128)(2,1)S(1)}, bf16[9,64]{1,0:T(8,128)(2,1)}, u32[]{:S(2)}) copy-start(bf16[9,64]{1,0:T(8,128)(2,1)} %param.12) | copy-start | bytes 3460
  154.7 58.4 %copy-start.1 = (bf16[4,256,64]{1,2,0:T(8,128)(2,1)S(1)}, bf16[4,256,64]{1,2,0:T(8,128)(2,1)}, u32[]{:S(2)}) copy-start(bf16[4,256,64]{1,2,0:T(8,128)(2,1)} %param.11) | copy-start | bytes 393220
  154.7 55.8 %all-gather.2.cloned.1.call-start = ((), (), s32[]{:S(2)}) async-start(), calls=%async_computation.4 | async-start | bytes 1572864 | tf_op jit(solution)/shard_map/all_gather | solution.py:90
  214.1 3.5 %collective-permute-start = (bf16[2,32,64]{2,1,0:T(8,128)(2,1)S(1)}, bf16[2,32,64]{2,1,0:T(8,128)(2,1)S(1)}, u32[]{:S(2)}, u32[]{:S(2)}) collective-permute-start(bf16[2,32,64]{2,1,0:T(8,128)(2,1)S(1)} %get-tuple-element.52), channel_id=1, source_target_pairs={{0,1},{1,8},{8,9},{9,16},{16,17},{17,24},{24,25},{2,3},{3,10},{10,... | collective-permute-start | bytes 24584 | tf_op jit(solution)/shard_map/ppermute | solution.py:18
  216.2 4.2 %collective-permute-start.1 = (bf16[2,32,64]{2,1,0:T(8,128)(2,1)S(1)}, bf16[2,32,64]{2,1,0:T(8,128)(2,1)S(1)}, u32[]{:S(2)}, u32[]{:S(2)}) collective-permute-start(bf16[2,32,64]{2,1,0:T(8,128)(2,1)S(1)} %get-tuple-element.53), channel_id=1, source_target_pairs={{1,0},{8,1},{9,8},{16,9},{17,16},{24,17},{25,24},{3,2},{10,3},{11,... | collective-permute-start | bytes 24584 | tf_op jit(solution)/shard_map/ppermute | solution.py:19
Sparse Core Ops, SparseCore 0:
  154.9 44.5 all-reduce.2
  201.8 8.7 all-gather.1
where the time goes:
time: 241 us; the launch traced here: 240 us
  waiting for transfers between devices  93.1 us (39%)
  local copies, waits for them, and re-layouts  45 us (19%)
  other arithmetic  27.5 us (11%)
  matrix products  24.4 us (10%)
  blocking collectives  21.1 us (9%)
  starting transfers between devices  14.9 us (6%)
  between operations  13.6 us (6%)
    all_to_all x1, waiting for transfers between devices, local(): lax.all_to_all(sent_values, 'tile', split_axis=0, concat_axis=0, tiled=True)  47.6 us
    psum x1, waiting for transfers between devices, local(): lax.psum(totals.astype(jnp.bfloat16), 'chan').astype(jnp.float32)  34.5 us
    dot_general x16, matrix products, grid_block(): jnp.dot(matches.astype(jnp.bfloat16), arrived_values, preferred_element_t...  23.7 us
    scatter x1, local copies, waits for them, and re-layouts, pack_rows(): jnp.full((tile_count * capacity,), -1, jnp.int32).at[slot_index].set(placed)  16.3 us
    scatter x1, local copies, waits for them, and re-layouts, pack_rows(): jnp.zeros((tile_count * capacity, width), jnp.bfloat16).at[slot_index]  12.4 us
    add x16, other arithmetic, grid_block(): cell_ids = first_cell + lax.iota(jnp.int32, 128)  11 us
    all_to_all x1, blocking collectives, local(): lax.all_to_all(outgoing, 'tile', split_axis=0, concat_axis=0, tiled=True)  11 us
    dynamic_slice x16, local copies, waits for them, and re-layouts, local(): lax.map(lambda first_cell: grid_block(arrived_values, arrived_cells, firs...  10.7 us
  transfers between devices with their start and end apart: 6, of which 4 were waited for; matrix products, arithmetic and copies ran while one was open for 6% of the time, Pallas kernels for 0%

commit v1 on v0

--- a/solution.py
+++ b/solution.py
@@ -80,7 +80,7 @@
     totals = totals.reshape(cell_count, V)
     counts = counts.reshape(cell_count)
     totals, counts = (
-        lax.psum(totals.astype(jnp.bfloat16), "chan").astype(jnp.float32),
+        jnp.sum(lax.all_gather(totals.astype(jnp.bfloat16), "chan"), axis=0).astype(jnp.float32),
         lax.psum(counts.astype(jnp.bfloat16), "chan").astype(jnp.float32),
     )
     means = (totals / jnp.maximum(counts, 1.0)[:, None]).astype(jnp.bfloat16)

time: 241 us -> 232 us (0.963)
  waiting for transfers between devices: 93.1 us -> 82.9 us
    psum x1 -> x0, waiting for transfers between devices: 34.5 us -> none  [local(): lax.psum(totals.astype(jnp.bfloat16), 'chan').astype(jnp.float32)]
    all_gather x0 -> x1, waiting for transfers between devices: none -> 24.3 us  [local(): lax.all_gather(totals.astype(jnp.bfloat16), 'chan')]
where the time goes in v1:
time: 232 us; the launch traced here: 231 us
  waiting for transfers between devices  82.9 us (36%)
  local copies, waits for them, and re-layouts  45 us (19%)
  other arithmetic  28.6 us (12%)
  matrix products  24.4 us (11%)
  blocking collectives  21 us (9%)
  starting transfers between devices  14.9 us (6%)
  between operations  13.6 us (6%)
    all_to_all x1, waiting for transfers between devices, local(): lax.all_to_all(sent_values, 'tile', split_axis=0, concat_axis=0, tiled=True)  47.6 us
    all_gather x1, waiting for transfers between devices, local(): lax.all_gather(totals.astype(jnp.bfloat16), 'chan')  24.3 us
    dot_general x16, matrix products, grid_block(): jnp.dot(matches.astype(jnp.bfloat16), arrived_values, preferred_element_t...  23.7 us
    scatter x1, local copies, waits for them, and re-layouts, pack_rows(): jnp.full((tile_count * capacity,), -1, jnp.int32).at[slot_index].set(placed)  16.3 us
    scatter x1, local copies, waits for them, and re-layouts, pack_rows(): jnp.zeros((tile_count * capacity, width), jnp.bfloat16).at[slot_index]  12.4 us
    add x16, other arithmetic, grid_block(): cell_ids = first_cell + lax.iota(jnp.int32, 128)  11 us
    all_to_all x1, blocking collectives, local(): lax.all_to_all(outgoing, 'tile', split_axis=0, concat_axis=0, tiled=True)  11 us
    dynamic_slice x16, local copies, waits for them, and re-layouts, local(): lax.map(lambda first_cell: grid_block(arrived_values, arrived_cells, firs...  10.7 us
  transfers between devices with their start and end apart: 6, of which 4 were waited for; matrix products, arithmetic and copies ran while one was open for 6% of the time, Pallas kernels for 0%

profile of v1, /device:TPU:0, one launch (start us, length us, event | category | flops | bytes accessed | tf_op | source)
XLA Modules:
  0.0 230.8 jit_solution(5552834944763612105)
XLA Ops:
  10.6 16.3 %scatter_custom_fusion = s32[8192]{0:T(1024)} fusion(s32[4096]{0:T(1024)S(1)} %bitcast.138, s32[4096]{0:T(1024)} %bitcast.142, s32[]{:T(128)} %constant.27.clone.1), kind=kCustom, calls=%fused_computation.78 | custom fusion | bytes 33280 | tf_op jit(solution)/shard_map/scatter | solution.py:31
  26.9 6.3 %all-to-all-start = ((s32[4,1,2048]{2,1,0:T(1,128)}), s32[4,1,2048]{2,1,0:T(1,128)S(1)}, u32[]{:S(2)}, u32[]{:S(2)}) async-start(s32[4,1,2048]{2,1,0:T(1,128)} %bitcast.10), calls=%async_computation | async-start | bytes 65536 | tf_op jit(solution)/shard_map/all_to_all | solution.py:71
  33.2 12.4 %scatter_custom_fusion.1 = bf16[8192,128]{1,0:T(8,128)(2,1)} fusion(s32[4096]{0:T(1024)S(1)} %bitcast.139, bf16[1,4096,128]{2,1,0:T(8,128)(2,1)S(1)} %copy-done, bf16[]{:T(256)} %constant.30.clone.1), kind=kCustom, calls=%fused_computation.17 | custom fusion | bytes 3145730 | tf_op jit(solution)/shard_map/scatter | solution.py:30
  45.6 5.1 %all-to-all-start.1 = ((bf16[4,2048,128]{2,1,0:T(8,128)(2,1)}), bf16[4,2048,128]{2,1,0:T(8,128)(2,1)S(1)}, u32[]{:S(2)}, u32[]{:S(2)}) async-start(bf16[4,2048,128]{2,1,0:T(8,128)(2,1)} %bitcast.12), calls=%async_computation.1 | async-start | bytes 4194304 | tf_op jit(solution)/shard_map/all_to_all | solution.py:70
  50.8 47.6 %all-to-all-done.1 = bf16[4,2048,128]{2,1,0:T(8,128)(2,1)S(1)} async-done(((bf16[4,2048,128]{2,1,0:T(8,128)(2,1)}), bf16[4,2048,128]{2,1,0:T(8,128)(2,1)S(1)}, u32[]{:S(2)}, u32[]{:S(2)}) %all-to-all-start.1) | async-done | bytes 2097184 | tf_op jit(solution)/shard_map/all_to_all | solution.py:70
  98.4 56.3 %while.12 = (s32[]{:T(128)}, bf16[16,128,128]{2,1,0:T(8,128)(2,1)}, bf16[16,128]{1,0:T(8,128)(2,1)S(1)}, s32[16]{0:T(128)S(1)}, s32[4,2048]{1,0:T(4,128)S(1)}, /...) while((s32[]{:T(128)}, bf16[16,128,128]{2,1,0:T(8,128)(2,1)}, bf16[16,128]{1,0:T(8,128)(2,1)S(1)}, ...), condition=%wide.region_7.8_spmd, body=%wide.region_5.7_spmd.sunk | while | flops 272629760 | bytes 2296681 | solution.py:77
  99.7 1.5 fusion.68
  103.3 1.5 fusion.68
  106.8 1.5 fusion.68
  117.3 1.5 fusion.68
  120.9 1.5 fusion.68
  124.4 1.5 fusion.68
  131.4 1.5 fusion.68
  134.9 1.5 fusion.68
  138.5 1.5 fusion.68
  145.5 1.5 fusion.68
  152.5 1.5 fusion.68
  154.8 10.0 %psum.7 = bf16[2048]{0:T(1024)(128)(2,1)S(1)} all-reduce(bf16[2048]{0:T(1024)(128)(2,1)S(1)} %bitcast.141), channel_id=1, replica_groups=mesh['tile'=4,'chan'=4,'tm'=2] {'chan'}, use_global_device_ids=true, to_apply=%region_9.10 | all-reduce | flops 2048 | bytes 8192 | tf_op jit(solution)/shard_map/psum | solution.py:84
  164.9 24.3 %all-gather.3.cloned.1.call-done = bf16[4,2048,128]{2,1,0:T(8,128)(2,1)} async-done(((bf16[1,2048,128]{2,1,0:T(8,128)(2,1)}), bf16[4,2048,128]{2,1,0:T(8,128)(2,1)}) %all-gather.3.cloned.1.call-update) | async-done | bytes 2097168 | tf_op jit(solution)/shard_map/all_gather | solution.py:83
  189.2 2.2 reduce_sum.45
  193.4 8.1 %all-gather.5.cloned.1.call-done = bf16[32,64,256]{2,1,0:T(8,128)(2,1)} async-done(((bf16[32,64,128]{2,1,0:T(8,128)(2,1)}), bf16[32,64,256]{2,1,0:T(8,128)(2,1)}) %all-gather.5.cloned.1.call-update) | async-done | bytes 1048592 | tf_op jit(solution)/shard_map/all_gather | solution.py:90
  205.0 2.2 collective-permute-start
  208.5 2.9 %collective-permute-done.1 = bf16[2,32,64]{2,1,0:T(8,128)(2,1)S(1)} collective-permute-done((bf16[2,32,64]{2,1,0:T(8,128)(2,1)S(1)}, bf16[2,32,64]{2,1,0:T(8,128)(2,1)S(1)}, u32[]{:S(2)}, u32[]{:S(2)}) %collective-permute-start.1) | collective-permute-done | bytes 8224 | tf_op jit(solution)/shard_map/ppermute | solution.py:19
  212.3 11.0 %all_to_all.22 = bf16[4,2,2048]{2,1,0:T(2,128)(2,1)S(1)} all-to-all(bf16[4,2,2048]{2,1,0:T(2,128)(2,1)S(1)} %reshape.230), channel_id=1, replica_groups=mesh['tile'=4,'chan'=4,'tm'=2] {'tile'}, dimensions={0} | all-to-all | bytes 65536 | tf_op jit(solution)/shard_map/all_to_all | solution.py:111
  (134 shorter events, 52.2 us)
Async XLA Ops:
  6.5 26.7 %copy-start = (bf16[1,4096,128]{2,1,0:T(8,128)(2,1)S(1)}, bf16[1,4096,128]{2,1,0:T(8,128)(2,1)}, u32[]{:S(2)}) copy-start(bf16[1,4096,128]{2,1,0:T(8,128)(2,1)} %param.8) | copy-start | bytes 3145732
  26.9 18.8 %all-to-all-start = ((s32[4,1,2048]{2,1,0:T(1,128)}), s32[4,1,2048]{2,1,0:T(1,128)S(1)}, u32[]{:S(2)}, u32[]{:S(2)}) async-start(s32[4,1,2048]{2,1,0:T(1,128)} %bitcast.10), calls=%async_computation | async-start | bytes 65536 | tf_op jit(solution)/shard_map/all_to_all | solution.py:71
  45.6 52.7 %all-to-all-start.1 = ((bf16[4,2048,128]{2,1,0:T(8,128)(2,1)}), bf16[4,2048,128]{2,1,0:T(8,128)(2,1)S(1)}, u32[]{:S(2)}, u32[]{:S(2)}) async-start(bf16[4,2048,128]{2,1,0:T(8,128)(2,1)} %bitcast.12), calls=%async_computation.1 | async-start | bytes 4194304 | tf_op jit(solution)/shard_map/all_to_all | solution.py:70
  50.7 138.4 %all-gather.3.cloned.1.call-start = ((), (), s32[]{:S(2)}) async-start(), calls=%async_computation.3 | async-start | bytes 2621440 | tf_op jit(solution)/shard_map/all_gather | solution.py:83
  154.7 46.8 %all-gather.5.cloned.1.call-start = ((), (), s32[]{:S(2)}) async-start(), calls=%async_computation.4 | async-start | bytes 1572864 | tf_op jit(solution)/shard_map/all_gather | solution.py:90
  164.9 28.5 %copy-start.2 = (bf16[9,64]{1,0:T(8,128)(2,1)S(1)}, bf16[9,64]{1,0:T(8,128)(2,1)}, u32[]{:S(2)}) copy-start(bf16[9,64]{1,0:T(8,128)(2,1)} %param.12) | copy-start | bytes 3460
  191.3 12.7 %copy-start.1 = (bf16[4,256,64]{1,2,0:T(8,128)(2,1)S(1)}, bf16[4,256,64]{1,2,0:T(8,128)(2,1)}, u32[]{:S(2)}) copy-start(bf16[4,256,64]{1,2,0:T(8,128)(2,1)} %param.11) | copy-start | bytes 393220
  205.0 3.5 %collective-permute-start = (bf16[2,32,64]{2,1,0:T(8,128)(2,1)S(1)}, bf16[2,32,64]{2,1,0:T(8,128)(2,1)S(1)}, u32[]{:S(2)}, u32[]{:S(2)}) collective-permute-start(bf16[2,32,64]{2,1,0:T(8,128)(2,1)S(1)} %get-tuple-element.52), channel_id=1, source_target_pairs={{0,1},{1,8},{8,9},{9,16},{16,17},{17,24},{24,25},{2,3},{3,10},{10,... | collective-permute-start | bytes 24584 | tf_op jit(solution)/shard_map/ppermute | solution.py:18
  207.1 4.2 %collective-permute-start.1 = (bf16[2,32,64]{2,1,0:T(8,128)(2,1)S(1)}, bf16[2,32,64]{2,1,0:T(8,128)(2,1)S(1)}, u32[]{:S(2)}, u32[]{:S(2)}) collective-permute-start(bf16[2,32,64]{2,1,0:T(8,128)(2,1)S(1)} %get-tuple-element.53), channel_id=1, source_target_pairs={{1,0},{8,1},{9,8},{16,9},{17,16},{24,17},{25,24},{3,2},{10,3},{11,... | collective-permute-start | bytes 24584 | tf_op jit(solution)/shard_map/ppermute | solution.py:19
Sparse Core Ops, SparseCore 0:
  154.8 34.2 all-gather.2
  192.7 8.7 all-gather.4
